TPU v7x, 32 devices: a whole 2x2x4 slice. The times are simulated.
32 devices in a mesh: dp: 8 (over z, y), rep: 4 (over x, core).
Axes of the slice: x: 2, y: 2, z: 4, core: 2. Of those that a mesh axis runs over, the one named last changes fastest.
Arguments:
- circuits: bfloat16 [8192, 1024], P(('dp', 'rep')), may hold values from -2.65 to 2.65
- records: bfloat16 [8192, 1024], P(('dp', 'rep')), may hold values from -0.25 to 0.25
- record_gain: float32 [1024], replicated, may hold values from 0.5 to 2
- log_scale: float32 [1], replicated, may hold values from 1.6 to 2.4
- logit_bias: float32 [1], replicated, may hold values from -3 to -1
- hard_ids: int32 [8192, 16], P(('dp', 'rep')), may hold values from -1 to 8191, as said below
Outputs:
- grad_circuits: float32 [8192, 1024], P(('dp', 'rep'))
- grad_records: float32 [8192, 1024], P(('dp', 'rep'))
- grad_gain: float32 [1024], replicated
- statistics: float32 [2], replicated
- mean_loss: float32 [1], replicated
Inputs may be any that keep to these rules, and one draw needn't show every extreme that they name: `hard_ids`: every entry that is not -1 names a row held by a device with the same dp index as the pair's device (the same value of row // 1024). Over the 256 pairs of one device, at most 16 entries name rows of any one device, and in each dp index one device is named exactly 16 times by every device of that dp index.
All inputs are finite; a program needn't handle non-finite values.
Results may differ from a plain program's by a relative error of at most 0.0043.
Values may be sent and summed in bfloat16 or wider, within the bound.
A program may use at most 64 MiB of HBM per device.

v0:
```python
import jax
import jax.numpy as jnp
from jax import lax
from jax.sharding import PartitionSpec as P

HOPS = 4
EPSILON = 1e-06


def shifted(value, axis, steps):
    count = lax.axis_size(axis)
    pairs = [(source, (source + steps) % count) for source in range(count)]
    return lax.ppermute(value, axis, pairs)


def unit_rows(values):
    sq_total = jnp.sum(values * values, axis=-1, keepdims=True)
    lengths = jnp.sqrt(sq_total + EPSILON)
    return (values / lengths, lengths)


def transposed_product(left, right):
    return lax.dot_general(
        left, right, (((0,), (0,)), ((), ())), preferred_element_type=jnp.float32
    )


def score_tile(circ_block, rec_block, multiplier, bias_value, own_block):
    products = lax.dot_general(
        circ_block, rec_block, (((1,), (1,)), ((), ())), preferred_element_type=jnp.float32
    )
    scores = products * multiplier + bias_value
    weights = jax.nn.sigmoid(scores)
    losses = jax.nn.softplus(scores)
    if own_block:
        tile_rows = scores.shape[0]
        diag_mask = (
            lax.broadcasted_iota(jnp.int32, (tile_rows, tile_rows), 0)
            == lax.broadcasted_iota(jnp.int32, (tile_rows, tile_rows), 1)
        ).astype(jnp.float32)
        weights = weights - diag_mask
        losses = losses - scores * diag_mask
    summary = jnp.stack(
        [jnp.sum(weights * (scores - bias_value)), jnp.sum(weights), jnp.sum(losses)]
    )
    return (weights.astype(jnp.bfloat16), summary)


def tile_terms(circ_block, rec_block, multiplier, bias_value):
    products = lax.dot_general(
        circ_block, rec_block, (((1,), (1,)), ((), ())), preferred_element_type=jnp.float32
    )
    return products * multiplier + bias_value


def per_device(circuits, records, record_gain, log_scale, logit_bias, hard_ids):
    pair_rows = circuits.shape[0]
    list_width = hard_ids.shape[1]
    rep_count = lax.axis_size("rep")
    loop_count = lax.axis_size("dp")
    circ_unit, circ_length = unit_rows(circuits.astype(jnp.float32))
    circ_emb = circ_unit.astype(jnp.bfloat16)
    rec_pre = records.astype(jnp.float32) * record_gain
    rec_unit, rec_length = unit_rows(rec_pre)
    rec_emb = rec_unit.astype(jnp.bfloat16)
    multiplier = jnp.exp(log_scale[0])
    bias_value = logit_bias[0]
    even = lax.axis_index("dp") % 2 == 0
    swap = [(source, source ^ 1) for source in range(loop_count)]
    rec2 = shifted(rec_emb, "dp", -2)
    circ2 = shifted(circ_emb, "dp", 2)
    rec4 = shifted(rec2, "dp", -2)
    circ4 = shifted(circ2, "dp", 2)
    rec1 = lax.ppermute(jnp.where(even, rec2, rec_emb), "dp", swap)
    circ1 = lax.ppermute(jnp.where(even, circ_emb, circ2), "dp", swap)
    rec3 = lax.ppermute(jnp.where(even, rec4, rec2), "dp", swap)
    circ3 = lax.ppermute(jnp.where(even, circ2, circ4), "dp", swap)
    own_weights, summary = score_tile(circ_emb, rec_emb, multiplier, bias_value, True)
    grad_circ = jnp.dot(own_weights, rec_emb, preferred_element_type=jnp.float32)
    grad_rec = transposed_product(own_weights, circ_emb)
    everyone = lax.all_gather(rec_emb, "rep", axis=0, tiled=True)
    first_row = lax.axis_index("dp") * rep_count * pair_rows
    columns = lax.broadcasted_iota(jnp.int32, (pair_rows, rep_count * pair_rows), 1) + first_row
    times = jnp.zeros(columns.shape, jnp.float32)
    for entry in range(list_width):
        times = times + (hard_ids[:, entry][:, None] == columns).astype(jnp.float32)
    for visitor, guest in ((rec2, circ2), (rec1, circ1), (rec4, circ4), (rec3, circ3)):
        weights, portion = score_tile(circ_emb, visitor, multiplier, bias_value, False)
        grad_circ = grad_circ + jnp.dot(weights, visitor, preferred_element_type=jnp.float32)
        summary = summary + portion
        scores = tile_terms(guest, rec_emb, multiplier, bias_value)
        weights = jax.nn.sigmoid(scores).astype(jnp.bfloat16)
        grad_rec = grad_rec + transposed_product(weights, guest)
    scores = tile_terms(circ_emb, everyone, multiplier, bias_value)
    sigmoids = jax.nn.sigmoid(scores)
    weights = times * sigmoids
    narrow = (times * sigmoids.astype(jnp.bfloat16).astype(jnp.float32)).astype(jnp.bfloat16)
    hard_grad = jnp.dot(narrow, everyone, preferred_element_type=jnp.float32)
    summary = summary + jnp.stack(
        [
            jnp.sum(weights * (scores - bias_value)),
            jnp.sum(weights),
            jnp.sum(times * jax.nn.softplus(scores)),
        ]
    )
    grad_circ_emb = multiplier * (grad_circ + hard_grad)
    grad_rec_emb = multiplier * grad_rec
    grad_circuits = (
        grad_circ_emb - circ_unit * jnp.sum(circ_unit * grad_circ_emb, axis=-1, keepdims=True)
    ) / circ_length
    grad_pre = (
        grad_rec_emb - rec_unit * jnp.sum(rec_unit * grad_rec_emb, axis=-1, keepdims=True)
    ) / rec_length
    grad_records = grad_pre * record_gain
    gain_part = jnp.sum(records.astype(jnp.float32) * grad_pre, axis=0)
    gain_total, summary_total = lax.psum((gain_part, summary), ("dp", "rep"))
    pair_total = pair_rows * loop_count * rep_count
    statistics = jnp.stack([summary_total[0], summary_total[1]])
    mean_loss = jnp.stack([summary_total[2] / pair_total])
    return (grad_circuits, grad_records, gain_total, statistics, mean_loss)


def solution(mesh):
    placed = (P(("dp", "rep"), None), P(("dp", "rep"), None), P(), P(), P(), P(("dp", "rep"), None))
    return jax.shard_map(
        per_device,
        mesh=mesh,
        in_specs=placed,
        out_specs=(P(("dp", "rep"), None), P(("dp", "rep"), None), P(), P(), P()),
        check_vma=False,
    )
```

profile of v0, /device:TPU:0, one launch (start us, length us, event | category | flops | bytes accessed | tf_op | source)
XLA Modules:
  0.0 178.6 jit_solution(16136791953172690187)
XLA Ops:
  7.2 0.0 copy-start.2
  7.2 0.0 copy-start.12
  7.2 0.0 all-gather.2.cloned.1.call-start
  7.2 1.3 fusion.38
  8.6 2.0 %fusion.84 = bf16[256,1024]{1,0:T(8,128)(2,1)} fusion(f32[256]{0:T(256)S(1)} %add_sqrt_fusion, f32[1024]{0:T(1024)} %param.8, bf16[256,1024]{1,0:T(8,128)(2,1)} %param.7), kind=kLoop, calls=%fused_computation.140 | loop fusion | flops 1048576 | bytes 1053696 | tf_op jit(solution)/shard_map/convert_element_type | solution.py:65
  10.6 0.0 all-gather.2.cloned.1.call-update
  10.6 5.1 %collective-permute-start = (bf16[256,1024]{1,0:T(8,128)(2,1)}, bf16[256,1024]{1,0:T(8,128)(2,1)}, u32[]{:S(2)}, u32[]{:S(2)}) collective-permute-start(bf16[256,1024]{1,0:T(8,128)(2,1)} %fusion.84), channel_id=1, source_target_pairs={{0,24},{4,28},{8,0},{12,4},{16,8},{20,12},{24,16},{28,20},{1,25},{... | collective-permute-start | bytes 1572872 | tf_op jit(solution)/shard_map/ppermute | solution.py:13
  15.7 0.0 copy-done.2
  15.7 0.2 fusion.39
  15.9 0.2 fusion.83
  16.2 0.1 collective-permute-start.4
  16.9 0.0 copy-done.12
  17.7 0.0 copy-done
  17.7 1.2 multiply_reduce_fusion.8
  18.9 0.3 fusion.70
  19.2 1.3 fusion.68
  20.5 7.8 %collective-permute-done = bf16[256,1024]{1,0:T(8,128)(2,1)} collective-permute-done((bf16[256,1024]{1,0:T(8,128)(2,1)}, bf16[256,1024]{1,0:T(8,128)(2,1)}, u32[]{:S(2)}, u32[]{:S(2)}) %collective-permute-start) | collective-permute-done | bytes 524320 | tf_op jit(solution)/shard_map/ppermute | solution.py:13
  28.4 4.3 %collective-permute-start.2 = (bf16[256,1024]{1,0:T(8,128)(2,1)}, bf16[256,1024]{1,0:T(8,128)(2,1)}, u32[]{:S(2)}, u32[]{:S(2)}) collective-permute-start(bf16[256,1024]{1,0:T(8,128)(2,1)} %collective-permute-done), channel_id=1, source_target_pairs={{0,24},{4,28},{8,0},{12,4},{16,8},{20,12},{24,16},{28,20},{1,25},{... | collective-permute-start | bytes 1572872 | tf_op jit(solution)/shard_map/ppermute | solution.py:13
  32.6 7.8 %collective-permute-done.4 = bf16[256,1024]{1,0:T(8,128)(2,1)S(1)} collective-permute-done((bf16[256,1024]{1,0:T(8,128)(2,1)S(1)}, bf16[256,1024]{1,0:T(8,128)(2,1)S(1)}, u32[]{:S(2)}, u32[]{:S(2)}) %collective-permute-start.4) | collective-permute-done | bytes 524320 | tf_op jit(solution)/shard_map/ppermute | solution.py:13
  40.4 1.5 collective-permute-start.6
  42.0 3.1 %convolution_add_fusion.2 = f32[256,1024]{1,0:T(8,128)} fusion(f32[256,1024]{1,0:T(8,128)} %fusion.68, bf16[256,1024]{1,0:T(8,128)(2,1)S(1)} %collective-permute-done.4, bf16[256,1024]{1,0:T(8,128)(2,1)S(1)} %copy-done, f32[]{:T(128)} %bitcast.69, f32[]{:T(128)} %bitcast), kind=kOutput, calls=%fused_computation.5 | convolution fusion | flops 269090816 | bytes 3145736 | tf_op jit(solution)/shard_map/dot_general | solution.py:23
  45.1 0.0 copy-done.5
  45.1 2.2 %multiply_reduce_fusion.7 = (f32[]{:T(128)}, f32[]{:T(128)}, f32[]{:T(128)}, f32[256,256]{1,0:T(8,128)S(1)}) fusion(f32[]{:T(128)} %bitcast.74, f32[]{:T(128)} %bitcast, bf16[256,1024]{1,0:T(8,128)(2,1)S(1)} %fusion.83, bf16[256,1024]{1,0:T(8,128)(2,1)} %collective-permute-done), kind=kOutput, calls=%fused_computation.94 | convolution fusion | flops 135266304 | bytes 1310740 | tf_op jit(solution)/shard_map/dot_general | solution.py:29
  47.3 2.4 %convolution_add_fusion.5 = f32[256,1024]{1,0:T(8,128)} fusion(f32[256,1024]{1,0:T(8,128)S(1)} %fusion.70, bf16[256,1024]{1,0:T(8,128)(2,1)} %collective-permute-done, f32[256,256]{1,0:T(8,128)S(1)} %get-tuple-element.55), kind=kOutput, calls=%fused_computation.11 | convolution fusion | flops 134742016 | bytes 2883584 | tf_op jit(solution)/shard_map/dot_general | solution.py:89
  49.7 1.9 %collective-permute-done.2 = bf16[256,1024]{1,0:T(8,128)(2,1)} collective-permute-done((bf16[256,1024]{1,0:T(8,128)(2,1)}, bf16[256,1024]{1,0:T(8,128)(2,1)}, u32[]{:S(2)}, u32[]{:S(2)}) %collective-permute-start.2) | collective-permute-done | bytes 524320 | tf_op jit(solution)/shard_map/ppermute | solution.py:13
  51.6 0.0 copy-done.1
  51.6 0.0 copy-done.11
  51.6 1.6 broadcast_select_fusion.3
  53.2 1.4 collective-permute-start.3
  54.6 0.7 collective-permute-start.1
  55.3 6.6 %collective-permute-done.6 = bf16[256,1024]{1,0:T(8,128)(2,1)} collective-permute-done((bf16[256,1024]{1,0:T(8,128)(2,1)S(1)}, bf16[256,1024]{1,0:T(8,128)(2,1)}, u32[]{:S(2)}, u32[]{:S(2)}) %collective-permute-start.6) | collective-permute-done | bytes 524320 | tf_op jit(solution)/shard_map/ppermute | solution.py:13
  61.9 1.2 broadcast_select_fusion.1
  63.0 2.6 %collective-permute-start.7 = (bf16[256,1024]{1,0:T(8,128)(2,1)S(1)}, bf16[256,1024]{1,0:T(8,128)(2,1)S(1)}, u32[]{:S(2)}, u32[]{:S(2)}) collective-permute-start(bf16[256,1024]{1,0:T(8,128)(2,1)S(1)} %get-tuple-element.28), channel_id=1, source_target_pairs={{0,4},{4,0},{8,12},{12,8},{16,20},{20,16},{24,28},{28,24},{1,5},{5... | collective-permute-start | bytes 1572872 | tf_op jit(solution)/shard_map/ppermute | solution.py:77
  65.6 0.0 collective-permute-start.5
  65.6 0.0 copy-done.6
  65.6 2.9 %multiply_reduce_fusion.5 = (f32[]{:T(128)}, f32[]{:T(128)}, f32[]{:T(128)}, f32[256,256]{1,0:T(8,128)}) fusion(f32[]{:T(128)} %bitcast.72, f32[]{:T(128)} %bitcast, bf16[256,1024]{1,0:T(8,128)(2,1)S(1)} %copy-done.6, bf16[256,1024]{1,0:T(8,128)(2,1)} %collective-permute-done.2), kind=kOutput, calls=%fused_computation.92 | convolution fusion | flops 135266304 | bytes 1310740 | tf_op jit(solution)/shard_map/dot_general | solution.py:29
  68.6 0.0 collective-permute-done.3
  68.6 1.2 multiply_reduce_fusion.4
  69.7 1.3 fusion.51
  71.0 8.3 %collective-permute-done.1 = bf16[256,1024]{1,0:T(8,128)(2,1)S(1)} collective-permute-done((bf16[256,1024]{1,0:T(8,128)(2,1)S(1)}, bf16[256,1024]{1,0:T(8,128)(2,1)S(1)}, u32[]{:S(2)}, u32[]{:S(2)}) %collective-permute-start.1) | collective-permute-done | bytes 524320 | tf_op jit(solution)/shard_map/ppermute | solution.py:74
  79.3 1.2 multiply_reduce_fusion.6
  80.5 0.0 copy-done.9
  80.5 10.0 %collective-permute-done.7 = bf16[256,1024]{1,0:T(8,128)(2,1)S(1)} collective-permute-done((bf16[256,1024]{1,0:T(8,128)(2,1)S(1)}, bf16[256,1024]{1,0:T(8,128)(2,1)S(1)}, u32[]{:S(2)}, u32[]{:S(2)}) %collective-permute-start.7) | collective-permute-done | bytes 524320 | tf_op jit(solution)/shard_map/ppermute | solution.py:77
  90.6 0.8 copy-done.13
  91.3 3.1 %fusion.37 = f32[256,1024]{1,0:T(8,128)} fusion(bf16[256,1024]{1,0:T(8,128)(2,1)} %copy-done.13, bf16[256,1024]{1,0:T(8,128)(2,1)S(1)} %copy-done, f32[]{:T(128)} %bitcast.76, f32[]{:T(128)} %bitcast), kind=kOutput, calls=%fused_computation.58 | convolution fusion | flops 268828672 | bytes 2097160 | tf_op jit(solution)/shard_map/dot_general | solution.py:23
  94.4 6.1 %collective-permute-done.5 = bf16[256,1024]{1,0:T(8,128)(2,1)S(1)} collective-permute-done((bf16[256,1024]{1,0:T(8,128)(2,1)}, bf16[256,1024]{1,0:T(8,128)(2,1)S(1)}, u32[]{:S(2)}, u32[]{:S(2)}) %collective-permute-start.5) | collective-permute-done | bytes 524320 | tf_op jit(solution)/shard_map/ppermute | solution.py:75
  100.5 0.0 copy-done.4
  100.5 1.9 %convolution_add_fusion.1 = f32[256,1024]{1,0:T(8,128)} fusion(f32[256,1024]{1,0:T(8,128)S(1)} %copy-done.4, bf16[256,1024]{1,0:T(8,128)(2,1)S(1)} %collective-permute-done.5, bf16[256,1024]{1,0:T(8,128)(2,1)S(1)} %copy-done, f32[]{:T(128)} %bitcast.68, f32[]{:T(128)} %bitcast), kind=kOutput, calls=%fused_computation.4 | convolution fusion | flops 269090816 | bytes 3145736 | tf_op jit(solution)/shard_map/dot_general | solution.py:23
  102.4 2.9 %multiply_reduce_fusion.1 = (f32[256]{0:T(256)S(1)}, f32[256,1024]{1,0:T(8,128)S(1)}) fusion(f32[256]{0:T(256)S(1)} %add_sqrt_fusion, f32[1024]{0:T(1024)S(1)} %copy-done.11, bf16[256,1024]{1,0:T(8,128)(2,1)S(1)} %copy-done.1, f32[256,1024]{1,0:T(8,128)} %fusion.37, f32[256,1024]{1,0:T(8,128)} %convolution_add_fusion.1, ...), kind=kOutput, calls=%fused_computation.66 | convolution fusion | flops 270925568 | bytes 4724744 | tf_op jit(solution)/shard_map/dot_general | solution.py:23
  105.3 0.0 copy-start.10
  105.3 0.4 fusion.40
  105.6 0.0 copy-start.7
  105.6 1.1 broadcast_multiply_fusion
  106.7 0.0 copy-done.3
  106.7 0.0 copy-done.10
  106.7 0.3 convolution_add_fusion.4
  107.1 0.0 all-gather.2.cloned.1.call-done
  107.1 5.2 %multiply_reduce_fusion = (f32[]{:T(128)}, f32[]{:T(128)}, f32[]{:T(128)}, f32[256,1024]{1,0:T(8,128)S(1)}) fusion(f32[]{:T(128)} %bitcast.70, s32[256]{0:T(256)S(1)} %bitcast.106, s32[256]{0:T(256)S(1)} %bitcast.108, s32[256]{0:T(256)S(1)} %bitcast.80, s32[256]{0:T(256)S(1)} %bitcast.82, s32[256]{0:T(256)S(1)} %bitcast.84, s32[256]{0:T(256)S(1)} %bitcast.86, ...), kind=kOutput, calls=%fused_computation.64 | convolution fusion | flops 553910272 | bytes 3690516 | tf_op jit(solution)/shard_map/dot_general | solution.py:50
  112.3 11.1 %fusion.74 = f32[3]{0:T(128)S(1)} fusion(f32[1]{0:T(128)} %bitcast.32, f32[1]{0:T(128)} %bitcast.31, f32[1]{0:T(128)} %bitcast.30, f32[1]{0:T(128)} %bitcast.35, f32[1]{0:T(128)} %bitcast.34, f32[1]{0:T(128)} %bitcast.33, f32[1]{0:T(128)} %bitcast.29, f32[1]{0:T(128)} %bitcast.28, f32[1]{0:T(128)} %bitcast.27, f32[1]{0:T(128)} %bitcast.26, f32[1]{0:T(128)} %bitcast.25, ...), kind=kLoop, calls=%fused_computation.130 | loop fusion | flops 51 | bytes 84 | tf_op jit(solution)/shard_map/add | solution.py:99
  123.4 39.1 %all-reduce = (f32[1024]{0:T(1024)}, f32[3]{0:T(128)S(1)}) all-reduce(f32[1024]{0:T(1024)S(1)} %get-tuple-element.25, f32[3]{0:T(128)S(1)} %fusion.74), channel_id=1, replica_groups=mesh['dp'=8,'rep'=4] {'dp','rep'}, use_global_device_ids=true, to_apply=%region_5.6 | all-reduce | flops 1027 | bytes 8216 | tf_op jit(solution)/shard_map/psum | solution.py:116
  162.5 0.6 slice.70
  163.1 4.0 %fusion.43 = f32[256,1024]{1,0:T(8,128)S(1)} fusion(bf16[1024,1024]{1,0:T(8,128)(2,1)} %all-gather.2.cloned.1.call-done, f32[256,1024]{1,0:T(8,128)S(1)} %get-tuple-element.52, s32[1024]{0:T(1024)S(1)} %iota_add_fusion, s32[256]{0:T(256)S(1)} %bitcast.107, s32[256]{0:T(256)S(1)} %bitcast.109, s32[256]{0:T(256)S(1)} %bitcast.81, s32[256]{0:T(256)S(1)} %bitcast.83, ...), kind=kOutput, calls=%fused_computation.77 | convolution fusion | flops 551026688 | bytes 4214784 | tf_op jit(solution)/shard_map/dot_general | solution.py:98
  167.2 1.6 multiply_reduce_fusion.2
  168.8 1.2 subtract_divide_fusion.1
  (20 shorter events, 0.1 us)
Async XLA Ops:
  7.2 8.6 %copy-start.2 = (bf16[256,1024]{1,0:T(8,128)(2,1)S(1)}, bf16[256,1024]{1,0:T(8,128)(2,1)}, u32[]{:S(2)}) copy-start(bf16[256,1024]{1,0:T(8,128)(2,1)} %param.6) | copy-start | bytes 1572868
  7.2 9.7 %copy-start.12 = (s32[256,16]{0,1:T(8,128)S(1)}, s32[256,16]{0,1:T(8,128)}, u32[]{:S(2)}) copy-start(s32[256,16]{0,1:T(8,128)} %param.11) | copy-start | bytes 49156
  7.2 99.9 %all-gather.2.cloned.1.call-start = ((), (), s32[]{:S(2)}) async-start(), calls=%async_computation | async-start | bytes 2621440 | tf_op jit(solution)/shard_map/all_gather | solution.py:81
  10.6 7.1 %copy-start = (bf16[256,1024]{1,0:T(8,128)(2,1)S(1)}, bf16[256,1024]{1,0:T(8,128)(2,1)}, u32[]{:S(2)}) copy-start(bf16[256,1024]{1,0:T(8,128)(2,1)} %fusion.84) | copy-start | bytes 1572868
  10.6 17.7 %collective-permute-start = (bf16[256,1024]{1,0:T(8,128)(2,1)}, bf16[256,1024]{1,0:T(8,128)(2,1)}, u32[]{:S(2)}, u32[]{:S(2)}) collective-permute-start(bf16[256,1024]{1,0:T(8,128)(2,1)} %fusion.84), channel_id=1, source_target_pairs={{0,24},{4,28},{8,0},{12,4},{16,8},{20,12},{24,16},{28,20},{1,25},{... | collective-permute-start | bytes 1572872 | tf_op jit(solution)/shard_map/ppermute | solution.py:13
  16.1 28.9 %copy-start.5 = (bf16[256,1024]{1,0:T(8,128)(2,1)}, bf16[256,1024]{1,0:T(8,128)(2,1)S(1)}, u32[]{:S(2)}) copy-start(bf16[256,1024]{1,0:T(8,128)(2,1)S(1)} %fusion.83) | copy-start | bytes 1572868
  16.2 24.3 %collective-permute-start.4 = (bf16[256,1024]{1,0:T(8,128)(2,1)S(1)}, bf16[256,1024]{1,0:T(8,128)(2,1)S(1)}, u32[]{:S(2)}, u32[]{:S(2)}) collective-permute-start(bf16[256,1024]{1,0:T(8,128)(2,1)S(1)} %fusion.83), channel_id=1, source_target_pairs={{0,8},{4,12},{8,16},{12,20},{16,24},{20,28},{24,0},{28,4},{1,9},{5... | collective-permute-start | bytes 1572872 | tf_op jit(solution)/shard_map/ppermute | solution.py:13
  28.4 23.2 %collective-permute-start.2 = (bf16[256,1024]{1,0:T(8,128)(2,1)}, bf16[256,1024]{1,0:T(8,128)(2,1)}, u32[]{:S(2)}, u32[]{:S(2)}) collective-permute-start(bf16[256,1024]{1,0:T(8,128)(2,1)} %collective-permute-done), channel_id=1, source_target_pairs={{0,24},{4,28},{8,0},{12,4},{16,8},{20,12},{24,16},{28,20},{1,25},{... | collective-permute-start | bytes 1572872 | tf_op jit(solution)/shard_map/ppermute | solution.py:13
  40.4 21.4 %collective-permute-start.6 = (bf16[256,1024]{1,0:T(8,128)(2,1)S(1)}, bf16[256,1024]{1,0:T(8,128)(2,1)}, u32[]{:S(2)}, u32[]{:S(2)}) collective-permute-start(bf16[256,1024]{1,0:T(8,128)(2,1)S(1)} %collective-permute-done.4), channel_id=1, source_target_pairs={{0,8},{4,12},{8,16},{12,20},{16,24},{20,28},{24,0},{28,4},{1,9},{5... | collective-permute-start | bytes 1572872 | tf_op jit(solution)/shard_map/ppermute | solution.py:13
  47.3 4.3 %copy-start.1 = (bf16[256,1024]{1,0:T(8,128)(2,1)S(1)}, bf16[256,1024]{1,0:T(8,128)(2,1)}, u32[]{:S(2)}) copy-start(bf16[256,1024]{1,0:T(8,128)(2,1)} %param.7) | copy-start | bytes 1572868
  47.3 4.3 %copy-start.11 = (f32[1024]{0:T(1024)S(1)}, f32[1024]{0:T(1024)}, u32[]{:S(2)}) copy-start(f32[1024]{0:T(1024)} %param.8) | copy-start | bytes 12292
  49.7 16.0 %copy-start.6 = (bf16[256,1024]{1,0:T(8,128)(2,1)S(1)}, bf16[256,1024]{1,0:T(8,128)(2,1)}, u32[]{:S(2)}) copy-start(bf16[256,1024]{1,0:T(8,128)(2,1)} %copy-done.5) | copy-start | bytes 1572868
  53.2 15.4 %collective-permute-start.3 = (bf16[256,1024]{1,0:T(8,128)(2,1)S(1)}, bf16[256,1024]{1,0:T(8,128)(2,1)S(1)}, u32[]{:S(2)}, u32[]{:S(2)}) collective-permute-start(bf16[256,1024]{1,0:T(8,128)(2,1)S(1)} %get-tuple-element.30), channel_id=1, source_target_pairs={{0,4},{4,0},{8,12},{12,8},{16,20},{20,16},{24,28},{28,24},{1,5},{5... | collective-permute-start | bytes 1572872 | tf_op jit(solution)/shard_map/ppermute | solution.py:76
  54.6 24.7 %collective-permute-start.1 = (bf16[256,1024]{1,0:T(8,128)(2,1)S(1)}, bf16[256,1024]{1,0:T(8,128)(2,1)S(1)}, u32[]{:S(2)}, u32[]{:S(2)}) collective-permute-start(bf16[256,1024]{1,0:T(8,128)(2,1)S(1)} %get-tuple-element.29), channel_id=1, source_target_pairs={{0,4},{4,0},{8,12},{12,8},{16,20},{20,16},{24,28},{28,24},{1,5},{5... | collective-permute-start | bytes 1572872 | tf_op jit(solution)/shard_map/ppermute | solution.py:74
  63.0 27.5 %collective-permute-start.7 = (bf16[256,1024]{1,0:T(8,128)(2,1)S(1)}, bf16[256,1024]{1,0:T(8,128)(2,1)S(1)}, u32[]{:S(2)}, u32[]{:S(2)}) collective-permute-start(bf16[256,1024]{1,0:T(8,128)(2,1)S(1)} %get-tuple-element.28), channel_id=1, source_target_pairs={{0,4},{4,0},{8,12},{12,8},{16,20},{20,16},{24,28},{28,24},{1,5},{5... | collective-permute-start | bytes 1572872 | tf_op jit(solution)/shard_map/ppermute | solution.py:77
  65.6 34.9 %collective-permute-start.5 = (bf16[256,1024]{1,0:T(8,128)(2,1)}, bf16[256,1024]{1,0:T(8,128)(2,1)S(1)}, u32[]{:S(2)}, u32[]{:S(2)}) collective-permute-start(bf16[256,1024]{1,0:T(8,128)(2,1)} %get-tuple-element.27), channel_id=1, source_target_pairs={{0,4},{4,0},{8,12},{12,8},{16,20},{20,16},{24,28},{28,24},{1,5},{5... | collective-permute-start | bytes 1572872 | tf_op jit(solution)/shard_map/ppermute | solution.py:75
  79.3 1.2 copy-start.9
  80.5 20.0 %copy-start.4 = (f32[256,1024]{1,0:T(8,128)S(1)}, f32[256,1024]{1,0:T(8,128)}, u32[]{:S(2)}) copy-start(f32[256,1024]{1,0:T(8,128)} %convolution_add_fusion.2) | copy-start | bytes 3145732
  90.5 0.8 copy-start.13
  105.2 1.5 copy-start.3
  105.3 1.5 copy-start.10
  105.6 1.5 copy-start.7
  162.5 4.6 %copy-start.14 = (f32[3]{0:T(128)}, f32[3]{0:T(128)S(1)}, u32[]{:S(2)}) copy-start(f32[3]{0:T(128)S(1)} %get-tuple-element.24) | copy-start | bytes 40
  163.1 4.1 %copy-start.8 = (f32[256,1024]{1,0:T(8,128)S(1)}, f32[256,1024]{1,0:T(8,128)}, u32[]{:S(2)}) copy-start(f32[256,1024]{1,0:T(8,128)} %fusion.51) | copy-start | bytes 3145732
  163.1 4.1 %copy-start.15 = (f32[256,256]{1,0:T(8,128)S(1)}, f32[256,256]{1,0:T(8,128)}, u32[]{:S(2)}) copy-start(f32[256,256]{1,0:T(8,128)} %get-tuple-element.53) | copy-start | bytes 786436
Sparse Core Ops, SparseCore 0:
  10.7 25.2 all-gather.1
where the time goes:
time: 179 us
  waiting for transfers between devices  48.6 us (27%)
  blocking collectives  39.1 us (22%)
  matrix products  36.1 us (20%)
  other arithmetic  20.3 us (11%)
  between operations  17.4 us (10%)
  starting transfers between devices  15.7 us (9%)
    psum x1, blocking collectives, per_device(): gain_total, summary_total = lax.psum((gain_part, summary), ('dp', 'rep'))  39.1 us
    ppermute x4, waiting for transfers between devices, shifted(): return lax.ppermute(value, axis, pairs)  24.2 us
    dot_general x5, matrix products, transposed_product(): lax.dot_general(left, right, (((0,), (0,)), ((), ())), preferred_element_...  12.3 us
    add x1, other arithmetic, per_device(): summary + jnp.stack([jnp.sum(weights * (scores - bias_value)), jnp.sum(we...  11.1 us
    ppermute x4, starting transfers between devices, shifted(): return lax.ppermute(value, axis, pairs)  11 us
    ppermute x1, waiting for transfers between devices, per_device(): circ3 = lax.ppermute(jnp.where(even, circ2, circ4), 'dp', swap)  10 us
    dot_general x5, matrix products, score_tile(): lax.dot_general(circ_block, rec_block, (((1,), (1,)), ((), ())), preferre...  8.68 us
    ppermute x1, waiting for transfers between devices, per_device(): rec1 = lax.ppermute(jnp.where(even, rec2, rec_emb), 'dp', swap)  8.29 us
  transfers between devices with their start and end apart: 9, of which 7 were waited for; matrix products, arithmetic and copies ran while one was open for 17% of the time, Pallas kernels for 0%

commit v1 on v0

--- a/solution.py
+++ b/solution.py
@@ -113,7 +113,10 @@
     ) / rec_length
     grad_records = grad_pre * record_gain
     gain_part = jnp.sum(records.astype(jnp.float32) * grad_pre, axis=0)
-    gain_total, summary_total = lax.psum((gain_part, summary), ("dp", "rep"))
+    place_slot = lambda inp, group_axis, shard_axis: lax.psum(
+        lax.psum(inp, group_axis), axis_name=shard_axis
+    )
+    gain_total, summary_total = place_slot((gain_part, summary), "rep", "dp")
     pair_total = pair_rows * loop_count * rep_count
     statistics = jnp.stack([summary_total[0], summary_total[1]])
     mean_loss = jnp.stack([summary_total[2] / pair_total])

time: 179 us -> 167 us (0.933)
  blocking collectives: 39.1 us -> 26.5 us
    psum x1 -> x2, blocking collectives: 39.1 us -> 26.5 us  [the longest x1 20.7 us: per_device(): lax.psum(lax.psum(inp, group_axis), axis_name=shard_axis)]
  transfers between devices with their start and end apart: 9 -> 9, of which waited for: 7 -> 7; matrix products, arithmetic and copies ran while one was open for 17% -> 18% of each run, Pallas kernels for 0% -> 0%
where the time goes in v1:
time: 167 us; the launch traced here: 166 us
  waiting for transfers between devices  48.6 us (29%)
  matrix products  36.1 us (22%)
  blocking collectives  26.5 us (16%)
  other arithmetic  20.3 us (12%)
  between operations  17.4 us (10%)
  starting transfers between devices  15.7 us (9%)
    ppermute x4, waiting for transfers between devices, shifted(): return lax.ppermute(value, axis, pairs)  24.2 us
    psum x1, blocking collectives, per_device(): lax.psum(lax.psum(inp, group_axis), axis_name=shard_axis)  20.7 us
    dot_general x5, matrix products, transposed_product(): lax.dot_general(left, right, (((0,), (0,)), ((), ())), preferred_element_...  12.3 us
    add x1, other arithmetic, per_device(): summary + jnp.stack([jnp.sum(weights * (scores - bias_value)), jnp.sum(we...  11.1 us
    ppermute x4, starting transfers between devices, shifted(): return lax.ppermute(value, axis, pairs)  11 us
    ppermute x1, waiting for transfers between devices, per_device(): circ3 = lax.ppermute(jnp.where(even, circ2, circ4), 'dp', swap)  10 us
    dot_general x5, matrix products, score_tile(): lax.dot_general(circ_block, rec_block, (((1,), (1,)), ((), ())), preferre...  8.68 us
    ppermute x1, waiting for transfers between devices, per_device(): rec1 = lax.ppermute(jnp.where(even, rec2, rec_emb), 'dp', swap)  8.29 us
  transfers between devices with their start and end apart: 9, of which 7 were waited for; matrix products, arithmetic and copies ran while one was open for 18% of the time, Pallas kernels for 0%

profile of v1, /device:TPU:0, one launch (start us, length us, event | category | flops | bytes accessed | tf_op | source)
XLA Modules:
  0.0 166.0 jit_solution(106100266629176088)
XLA Ops:
  7.2 0.0 copy-start.2
  7.2 0.0 copy-start.12
  7.2 0.0 all-gather.2.cloned.1.call-start
  7.2 1.3 fusion.38
  8.6 2.0 %fusion.84 = bf16[256,1024]{1,0:T(8,128)(2,1)} fusion(f32[256]{0:T(256)S(1)} %add_sqrt_fusion, f32[1024]{0:T(1024)} %param.8, bf16[256,1024]{1,0:T(8,128)(2,1)} %param.7), kind=kLoop, calls=%fused_computation.140 | loop fusion | flops 1048576 | bytes 1053696 | tf_op jit(solution)/shard_map/convert_element_type | solution.py:65
  10.6 0.0 all-gather.2.cloned.1.call-update
  10.6 5.1 %collective-permute-start = (bf16[256,1024]{1,0:T(8,128)(2,1)}, bf16[256,1024]{1,0:T(8,128)(2,1)}, u32[]{:S(2)}, u32[]{:S(2)}) collective-permute-start(bf16[256,1024]{1,0:T(8,128)(2,1)} %fusion.84), channel_id=1, source_target_pairs={{0,24},{4,28},{8,0},{12,4},{16,8},{20,12},{24,16},{28,20},{1,25},{... | collective-permute-start | bytes 1572872 | tf_op jit(solution)/shard_map/ppermute | solution.py:13
  15.7 0.0 copy-done.2
  15.7 0.2 fusion.39
  15.9 0.2 fusion.83
  16.2 0.1 collective-permute-start.4
  16.9 0.0 copy-done.12
  17.7 0.0 copy-done
  17.7 1.2 multiply_reduce_fusion.8
  18.9 0.3 fusion.70
  19.2 1.3 fusion.68
  20.5 7.8 %collective-permute-done = bf16[256,1024]{1,0:T(8,128)(2,1)} collective-permute-done((bf16[256,1024]{1,0:T(8,128)(2,1)}, bf16[256,1024]{1,0:T(8,128)(2,1)}, u32[]{:S(2)}, u32[]{:S(2)}) %collective-permute-start) | collective-permute-done | bytes 524320 | tf_op jit(solution)/shard_map/ppermute | solution.py:13
  28.4 4.3 %collective-permute-start.2 = (bf16[256,1024]{1,0:T(8,128)(2,1)}, bf16[256,1024]{1,0:T(8,128)(2,1)}, u32[]{:S(2)}, u32[]{:S(2)}) collective-permute-start(bf16[256,1024]{1,0:T(8,128)(2,1)} %collective-permute-done), channel_id=1, source_target_pairs={{0,24},{4,28},{8,0},{12,4},{16,8},{20,12},{24,16},{28,20},{1,25},{... | collective-permute-start | bytes 1572872 | tf_op jit(solution)/shard_map/ppermute | solution.py:13
  32.6 7.8 %collective-permute-done.4 = bf16[256,1024]{1,0:T(8,128)(2,1)S(1)} collective-permute-done((bf16[256,1024]{1,0:T(8,128)(2,1)S(1)}, bf16[256,1024]{1,0:T(8,128)(2,1)S(1)}, u32[]{:S(2)}, u32[]{:S(2)}) %collective-permute-start.4) | collective-permute-done | bytes 524320 | tf_op jit(solution)/shard_map/ppermute | solution.py:13
  40.4 1.5 collective-permute-start.6
  42.0 3.1 %convolution_add_fusion.2 = f32[256,1024]{1,0:T(8,128)} fusion(f32[256,1024]{1,0:T(8,128)} %fusion.68, bf16[256,1024]{1,0:T(8,128)(2,1)S(1)} %collective-permute-done.4, bf16[256,1024]{1,0:T(8,128)(2,1)S(1)} %copy-done, f32[]{:T(128)} %bitcast.69, f32[]{:T(128)} %bitcast), kind=kOutput, calls=%fused_computation.5 | convolution fusion | flops 269090816 | bytes 3145736 | tf_op jit(solution)/shard_map/dot_general | solution.py:23
  45.1 0.0 copy-done.5
  45.1 2.2 %multiply_reduce_fusion.7 = (f32[]{:T(128)}, f32[]{:T(128)}, f32[]{:T(128)}, f32[256,256]{1,0:T(8,128)S(1)}) fusion(f32[]{:T(128)} %bitcast.74, f32[]{:T(128)} %bitcast, bf16[256,1024]{1,0:T(8,128)(2,1)S(1)} %fusion.83, bf16[256,1024]{1,0:T(8,128)(2,1)} %collective-permute-done), kind=kOutput, calls=%fused_computation.94 | convolution fusion | flops 135266304 | bytes 1310740 | tf_op jit(solution)/shard_map/dot_general | solution.py:29
  47.3 2.4 %convolution_add_fusion.5 = f32[256,1024]{1,0:T(8,128)} fusion(f32[256,1024]{1,0:T(8,128)S(1)} %fusion.70, bf16[256,1024]{1,0:T(8,128)(2,1)} %collective-permute-done, f32[256,256]{1,0:T(8,128)S(1)} %get-tuple-element.57), kind=kOutput, calls=%fused_computation.11 | convolution fusion | flops 134742016 | bytes 2883584 | tf_op jit(solution)/shard_map/dot_general | solution.py:89
  49.7 1.9 %collective-permute-done.2 = bf16[256,1024]{1,0:T(8,128)(2,1)} collective-permute-done((bf16[256,1024]{1,0:T(8,128)(2,1)}, bf16[256,1024]{1,0:T(8,128)(2,1)}, u32[]{:S(2)}, u32[]{:S(2)}) %collective-permute-start.2) | collective-permute-done | bytes 524320 | tf_op jit(solution)/shard_map/ppermute | solution.py:13
  51.6 0.0 copy-done.1
  51.6 0.0 copy-done.11
  51.6 1.6 broadcast_select_fusion.3
  53.2 1.4 collective-permute-start.3
  54.6 0.7 collective-permute-start.1
  55.3 6.6 %collective-permute-done.6 = bf16[256,1024]{1,0:T(8,128)(2,1)} collective-permute-done((bf16[256,1024]{1,0:T(8,128)(2,1)S(1)}, bf16[256,1024]{1,0:T(8,128)(2,1)}, u32[]{:S(2)}, u32[]{:S(2)}) %collective-permute-start.6) | collective-permute-done | bytes 524320 | tf_op jit(solution)/shard_map/ppermute | solution.py:13
  61.9 1.2 broadcast_select_fusion.1
  63.0 2.6 %collective-permute-start.7 = (bf16[256,1024]{1,0:T(8,128)(2,1)S(1)}, bf16[256,1024]{1,0:T(8,128)(2,1)S(1)}, u32[]{:S(2)}, u32[]{:S(2)}) collective-permute-start(bf16[256,1024]{1,0:T(8,128)(2,1)S(1)} %get-tuple-element.30), channel_id=1, source_target_pairs={{0,4},{4,0},{8,12},{12,8},{16,20},{20,16},{24,28},{28,24},{1,5},{5... | collective-permute-start | bytes 1572872 | tf_op jit(solution)/shard_map/ppermute | solution.py:77
  65.6 0.0 collective-permute-start.5
  65.6 0.0 copy-done.6
  65.6 2.9 %multiply_reduce_fusion.5 = (f32[]{:T(128)}, f32[]{:T(128)}, f32[]{:T(128)}, f32[256,256]{1,0:T(8,128)}) fusion(f32[]{:T(128)} %bitcast.72, f32[]{:T(128)} %bitcast, bf16[256,1024]{1,0:T(8,128)(2,1)S(1)} %copy-done.6, bf16[256,1024]{1,0:T(8,128)(2,1)} %collective-permute-done.2), kind=kOutput, calls=%fused_computation.92 | convolution fusion | flops 135266304 | bytes 1310740 | tf_op jit(solution)/shard_map/dot_general | solution.py:29
  68.6 0.0 collective-permute-done.3
  68.6 1.2 multiply_reduce_fusion.4
  69.7 1.3 fusion.51
  71.0 8.3 %collective-permute-done.1 = bf16[256,1024]{1,0:T(8,128)(2,1)S(1)} collective-permute-done((bf16[256,1024]{1,0:T(8,128)(2,1)S(1)}, bf16[256,1024]{1,0:T(8,128)(2,1)S(1)}, u32[]{:S(2)}, u32[]{:S(2)}) %collective-permute-start.1) | collective-permute-done | bytes 524320 | tf_op jit(solution)/shard_map/ppermute | solution.py:74
  79.3 1.2 multiply_reduce_fusion.6
  80.5 0.0 copy-done.9
  80.5 10.0 %collective-permute-done.7 = bf16[256,1024]{1,0:T(8,128)(2,1)S(1)} collective-permute-done((bf16[256,1024]{1,0:T(8,128)(2,1)S(1)}, bf16[256,1024]{1,0:T(8,128)(2,1)S(1)}, u32[]{:S(2)}, u32[]{:S(2)}) %collective-permute-start.7) | collective-permute-done | bytes 524320 | tf_op jit(solution)/shard_map/ppermute | solution.py:77
  90.6 0.8 copy-done.13
  91.3 3.1 %fusion.37 = f32[256,1024]{1,0:T(8,128)} fusion(bf16[256,1024]{1,0:T(8,128)(2,1)} %copy-done.13, bf16[256,1024]{1,0:T(8,128)(2,1)S(1)} %copy-done, f32[]{:T(128)} %bitcast.76, f32[]{:T(128)} %bitcast), kind=kOutput, calls=%fused_computation.58 | convolution fusion | flops 268828672 | bytes 2097160 | tf_op jit(solution)/shard_map/dot_general | solution.py:23
  94.4 6.1 %collective-permute-done.5 = bf16[256,1024]{1,0:T(8,128)(2,1)S(1)} collective-permute-done((bf16[256,1024]{1,0:T(8,128)(2,1)}, bf16[256,1024]{1,0:T(8,128)(2,1)S(1)}, u32[]{:S(2)}, u32[]{:S(2)}) %collective-permute-start.5) | collective-permute-done | bytes 524320 | tf_op jit(solution)/shard_map/ppermute | solution.py:75
  100.5 0.0 copy-done.4
  100.5 1.9 %convolution_add_fusion.1 = f32[256,1024]{1,0:T(8,128)} fusion(f32[256,1024]{1,0:T(8,128)S(1)} %copy-done.4, bf16[256,1024]{1,0:T(8,128)(2,1)S(1)} %collective-permute-done.5, bf16[256,1024]{1,0:T(8,128)(2,1)S(1)} %copy-done, f32[]{:T(128)} %bitcast.68, f32[]{:T(128)} %bitcast), kind=kOutput, calls=%fused_computation.4 | convolution fusion | flops 269090816 | bytes 3145736 | tf_op jit(solution)/shard_map/dot_general | solution.py:23
  102.4 2.9 %multiply_reduce_fusion.1 = (f32[256]{0:T(256)S(1)}, f32[256,1024]{1,0:T(8,128)S(1)}) fusion(f32[256]{0:T(256)S(1)} %add_sqrt_fusion, f32[1024]{0:T(1024)S(1)} %copy-done.11, bf16[256,1024]{1,0:T(8,128)(2,1)S(1)} %copy-done.1, f32[256,1024]{1,0:T(8,128)} %fusion.37, f32[256,1024]{1,0:T(8,128)} %convolution_add_fusion.1, ...), kind=kOutput, calls=%fused_computation.66 | convolution fusion | flops 270925568 | bytes 4724744 | tf_op jit(solution)/shard_map/dot_general | solution.py:23
  105.3 0.0 copy-start.10
  105.3 0.4 fusion.40
  105.6 0.0 copy-start.7
  105.6 1.1 broadcast_multiply_fusion
  106.7 0.0 copy-done.3
  106.7 0.3 convolution_add_fusion.4
  107.1 0.0 all-gather.2.cloned.1.call-done
  107.1 5.2 %multiply_reduce_fusion = (f32[]{:T(128)}, f32[]{:T(128)}, f32[]{:T(128)}, f32[256,1024]{1,0:T(8,128)S(1)}) fusion(f32[]{:T(128)} %bitcast.70, s32[256]{0:T(256)S(1)} %bitcast.106, s32[256]{0:T(256)S(1)} %bitcast.108, s32[256]{0:T(256)S(1)} %bitcast.80, s32[256]{0:T(256)S(1)} %bitcast.82, s32[256]{0:T(256)S(1)} %bitcast.84, s32[256]{0:T(256)S(1)} %bitcast.86, ...), kind=kOutput, calls=%fused_computation.64 | convolution fusion | flops 553910272 | bytes 3690516 | tf_op jit(solution)/shard_map/dot_general | solution.py:50
  112.3 11.1 %fusion.74 = f32[3]{0:T(128)S(1)} fusion(f32[1]{0:T(128)} %bitcast.32, f32[1]{0:T(128)} %bitcast.31, f32[1]{0:T(128)} %bitcast.30, f32[1]{0:T(128)} %bitcast.35, f32[1]{0:T(128)} %bitcast.34, f32[1]{0:T(128)} %bitcast.33, f32[1]{0:T(128)} %bitcast.29, f32[1]{0:T(128)} %bitcast.28, f32[1]{0:T(128)} %bitcast.27, f32[1]{0:T(128)} %bitcast.26, f32[1]{0:T(128)} %bitcast.25, ...), kind=kLoop, calls=%fused_computation.130 | loop fusion | flops 51 | bytes 84 | tf_op jit(solution)/shard_map/add | solution.py:99
  123.4 5.8 %all-reduce.1 = (f32[1024]{0:T(1024)S(1)}, f32[3]{0:T(128)S(1)}) all-reduce(f32[1024]{0:T(1024)S(1)} %get-tuple-element.27, f32[3]{0:T(128)S(1)} %fusion.74), channel_id=1, replica_groups=mesh['dp'=8,'rep'=4] {'rep'}, use_global_device_ids=true, to_apply=%region_5.6 | all-reduce | flops 1027 | bytes 8216 | tf_op jit(solution)/shard_map/psum | solution.py:117
  129.1 20.7 %all-reduce = (f32[1024]{0:T(1024)}, f32[3]{0:T(128)S(1)}) all-reduce(f32[1024]{0:T(1024)S(1)} %get-tuple-element.25, f32[3]{0:T(128)S(1)} %get-tuple-element.26), channel_id=1, replica_groups=mesh['dp'=8,'rep'=4] {'dp'}, use_global_device_ids=true, to_apply=%region_6.7 | all-reduce | flops 1027 | bytes 8216 | tf_op jit(solution)/shard_map/psum | solution.py:116
  149.8 0.6 slice.70
  150.4 4.0 %fusion.43 = f32[256,1024]{1,0:T(8,128)S(1)} fusion(bf16[1024,1024]{1,0:T(8,128)(2,1)} %all-gather.2.cloned.1.call-done, f32[256,1024]{1,0:T(8,128)S(1)} %get-tuple-element.54, s32[1024]{0:T(1024)S(1)} %iota_add_fusion, s32[256]{0:T(256)S(1)} %bitcast.107, s32[256]{0:T(256)S(1)} %bitcast.109, s32[256]{0:T(256)S(1)} %bitcast.81, s32[256]{0:T(256)S(1)} %bitcast.83, ...), kind=kOutput, calls=%fused_computation.77 | convolution fusion | flops 551026688 | bytes 4214784 | tf_op jit(solution)/shard_map/dot_general | solution.py:98
  154.5 1.6 multiply_reduce_fusion.2
  156.1 1.2 subtract_divide_fusion.1
  (21 shorter events, 0.1 us)
Async XLA Ops:
  7.2 8.6 %copy-start.2 = (bf16[256,1024]{1,0:T(8,128)(2,1)S(1)}, bf16[256,1024]{1,0:T(8,128)(2,1)}, u32[]{:S(2)}) copy-start(bf16[256,1024]{1,0:T(8,128)(2,1)} %param.6) | copy-start | bytes 1572868
  7.2 9.7 %copy-start.12 = (s32[256,16]{0,1:T(8,128)S(1)}, s32[256,16]{0,1:T(8,128)}, u32[]{:S(2)}) copy-start(s32[256,16]{0,1:T(8,128)} %param.11) | copy-start | bytes 49156
  7.2 99.9 %all-gather.2.cloned.1.call-start = ((), (), s32[]{:S(2)}) async-start(), calls=%async_computation | async-start | bytes 2621440 | tf_op jit(solution)/shard_map/all_gather | solution.py:81
  10.6 7.1 %copy-start = (bf16[256,1024]{1,0:T(8,128)(2,1)S(1)}, bf16[256,1024]{1,0:T(8,128)(2,1)}, u32[]{:S(2)}) copy-start(bf16[256,1024]{1,0:T(8,128)(2,1)} %fusion.84) | copy-start | bytes 1572868
  10.6 17.7 %collective-permute-start = (bf16[256,1024]{1,0:T(8,128)(2,1)}, bf16[256,1024]{1,0:T(8,128)(2,1)}, u32[]{:S(2)}, u32[]{:S(2)}) collective-permute-start(bf16[256,1024]{1,0:T(8,128)(2,1)} %fusion.84), channel_id=1, source_target_pairs={{0,24},{4,28},{8,0},{12,4},{16,8},{20,12},{24,16},{28,20},{1,25},{... | collective-permute-start | bytes 1572872 | tf_op jit(solution)/shard_map/ppermute | solution.py:13
  16.1 28.9 %copy-start.5 = (bf16[256,1024]{1,0:T(8,128)(2,1)}, bf16[256,1024]{1,0:T(8,128)(2,1)S(1)}, u32[]{:S(2)}) copy-start(bf16[256,1024]{1,0:T(8,128)(2,1)S(1)} %fusion.83) | copy-start | bytes 1572868
  16.2 24.3 %collective-permute-start.4 = (bf16[256,1024]{1,0:T(8,128)(2,1)S(1)}, bf16[256,1024]{1,0:T(8,128)(2,1)S(1)}, u32[]{:S(2)}, u32[]{:S(2)}) collective-permute-start(bf16[256,1024]{1,0:T(8,128)(2,1)S(1)} %fusion.83), channel_id=1, source_target_pairs={{0,8},{4,12},{8,16},{12,20},{16,24},{20,28},{24,0},{28,4},{1,9},{5... | collective-permute-start | bytes 1572872 | tf_op jit(solution)/shard_map/ppermute | solution.py:13
  28.4 23.2 %collective-permute-start.2 = (bf16[256,1024]{1,0:T(8,128)(2,1)}, bf16[256,1024]{1,0:T(8,128)(2,1)}, u32[]{:S(2)}, u32[]{:S(2)}) collective-permute-start(bf16[256,1024]{1,0:T(8,128)(2,1)} %collective-permute-done), channel_id=1, source_target_pairs={{0,24},{4,28},{8,0},{12,4},{16,8},{20,12},{24,16},{28,20},{1,25},{... | collective-permute-start | bytes 1572872 | tf_op jit(solution)/shard_map/ppermute | solution.py:13
  40.4 21.4 %collective-permute-start.6 = (bf16[256,1024]{1,0:T(8,128)(2,1)S(1)}, bf16[256,1024]{1,0:T(8,128)(2,1)}, u32[]{:S(2)}, u32[]{:S(2)}) collective-permute-start(bf16[256,1024]{1,0:T(8,128)(2,1)S(1)} %collective-permute-done.4), channel_id=1, source_target_pairs={{0,8},{4,12},{8,16},{12,20},{16,24},{20,28},{24,0},{28,4},{1,9},{5... | collective-permute-start | bytes 1572872 | tf_op jit(solution)/shard_map/ppermute | solution.py:13
  47.3 4.3 %copy-start.1 = (bf16[256,1024]{1,0:T(8,128)(2,1)S(1)}, bf16[256,1024]{1,0:T(8,128)(2,1)}, u32[]{:S(2)}) copy-start(bf16[256,1024]{1,0:T(8,128)(2,1)} %param.7) | copy-start | bytes 1572868
  47.3 4.3 %copy-start.11 = (f32[1024]{0:T(1024)S(1)}, f32[1024]{0:T(1024)}, u32[]{:S(2)}) copy-start(f32[1024]{0:T(1024)} %param.8) | copy-start | bytes 12292
  49.7 16.0 %copy-start.6 = (bf16[256,1024]{1,0:T(8,128)(2,1)S(1)}, bf16[256,1024]{1,0:T(8,128)(2,1)}, u32[]{:S(2)}) copy-start(bf16[256,1024]{1,0:T(8,128)(2,1)} %copy-done.5) | copy-start | bytes 1572868
  53.2 15.4 %collective-permute-start.3 = (bf16[256,1024]{1,0:T(8,128)(2,1)S(1)}, bf16[256,1024]{1,0:T(8,128)(2,1)S(1)}, u32[]{:S(2)}, u32[]{:S(2)}) collective-permute-start(bf16[256,1024]{1,0:T(8,128)(2,1)S(1)} %get-tuple-element.32), channel_id=1, source_target_pairs={{0,4},{4,0},{8,12},{12,8},{16,20},{20,16},{24,28},{28,24},{1,5},{5... | collective-permute-start | bytes 1572872 | tf_op jit(solution)/shard_map/ppermute | solution.py:76
  54.6 24.7 %collective-permute-start.1 = (bf16[256,1024]{1,0:T(8,128)(2,1)S(1)}, bf16[256,1024]{1,0:T(8,128)(2,1)S(1)}, u32[]{:S(2)}, u32[]{:S(2)}) collective-permute-start(bf16[256,1024]{1,0:T(8,128)(2,1)S(1)} %get-tuple-element.31), channel_id=1, source_target_pairs={{0,4},{4,0},{8,12},{12,8},{16,20},{20,16},{24,28},{28,24},{1,5},{5... | collective-permute-start | bytes 1572872 | tf_op jit(solution)/shard_map/ppermute | solution.py:74
  63.0 27.5 %collective-permute-start.7 = (bf16[256,1024]{1,0:T(8,128)(2,1)S(1)}, bf16[256,1024]{1,0:T(8,128)(2,1)S(1)}, u32[]{:S(2)}, u32[]{:S(2)}) collective-permute-start(bf16[256,1024]{1,0:T(8,128)(2,1)S(1)} %get-tuple-element.30), channel_id=1, source_target_pairs={{0,4},{4,0},{8,12},{12,8},{16,20},{20,16},{24,28},{28,24},{1,5},{5... | collective-permute-start | bytes 1572872 | tf_op jit(solution)/shard_map/ppermute | solution.py:77
  65.6 34.9 %collective-permute-start.5 = (bf16[256,1024]{1,0:T(8,128)(2,1)}, bf16[256,1024]{1,0:T(8,128)(2,1)S(1)}, u32[]{:S(2)}, u32[]{:S(2)}) collective-permute-start(bf16[256,1024]{1,0:T(8,128)(2,1)} %get-tuple-element.29), channel_id=1, source_target_pairs={{0,4},{4,0},{8,12},{12,8},{16,20},{20,16},{24,28},{28,24},{1,5},{5... | collective-permute-start | bytes 1572872 | tf_op jit(solution)/shard_map/ppermute | solution.py:75
  79.3 1.2 copy-start.9
  80.5 20.0 %copy-start.4 = (f32[256,1024]{1,0:T(8,128)S(1)}, f32[256,1024]{1,0:T(8,128)}, u32[]{:S(2)}) copy-start(f32[256,1024]{1,0:T(8,128)} %convolution_add_fusion.2) | copy-start | bytes 3145732
  90.5 0.8 copy-start.13
  105.2 1.5 copy-start.3
  105.3 1.5 copy-start.10
  105.6 1.5 copy-start.7
  149.8 4.6 %copy-start.14 = (f32[3]{0:T(128)}, f32[3]{0:T(128)S(1)}, u32[]{:S(2)}) copy-start(f32[3]{0:T(128)S(1)} %get-tuple-element.24) | copy-start | bytes 40
  150.4 4.1 %copy-start.8 = (f32[256,1024]{1,0:T(8,128)S(1)}, f32[256,1024]{1,0:T(8,128)}, u32[]{:S(2)}) copy-start(f32[256,1024]{1,0:T(8,128)} %fusion.51) | copy-start | bytes 3145732
  150.4 4.1 %copy-start.15 = (f32[256,256]{1,0:T(8,128)S(1)}, f32[256,256]{1,0:T(8,128)}, u32[]{:S(2)}) copy-start(f32[256,256]{1,0:T(8,128)} %get-tuple-element.55) | copy-start | bytes 786436
Sparse Core Ops, SparseCore 0:
  10.7 25.2 all-gather.1
